TPU v7x, 32 devices: a whole 2x2x4 slice. The times are simulated.
32 devices in a mesh: gx: 4 (over x, core), gy: 8 (over z, y).
Axes of the slice: x: 2, y: 2, z: 4, core: 2. Of those that a mesh axis runs over, the one named last changes fastest.
Arguments:
- queries: bfloat16 [256, 2560], P('gx'), may hold values from -8 to 8
- token_key_value: bfloat16 [256, 1024], P('gx'), may hold values from -6 to 6
- group_cached_keys: bfloat16 [4, 32768, 512], P('gx', 'gy'), may hold values from -8 to 8
- group_cached_values: bfloat16 [4, 32768, 512], P('gx', 'gy'), may hold values from -6 to 6
- owners: int32 [4, 32768], P('gx', 'gy'), may hold values from 0 to 63, never falling along the last dimension, each value on 1 to 16384 neighbouring positions
- out_weight: bfloat16 [2560, 2560], P(None, 'gy'), may hold values from -0.125 to 0.125
- residual: bfloat16 [256, 2560], P('gx', 'gy'), may hold values from -6 to 6
- norm_gain: bfloat16 [2560], P('gy'), may hold values from 0.099609375 to 1.8984375
- expert_ids: int32 [256, 6], replicated, may hold values from 0 to 63, all different within a row; in each aligned block of 64 rows (0 to 63, 64 to 127, ...) at most 12 rows name the same one
- gate_logits: float32 [256, 6], replicated, may hold values from -0.5 to 0.5
- w_gate_up: bfloat16 [64, 2560, 3072], P('gx', 'gy'), may hold values from -0.125 to 0.125
- w_down: bfloat16 [64, 1536, 2560], P('gx', None, 'gy'), may hold values from -0.15625 to 0.15625
Outputs:
- layer_out: float32 [256, 2560], P('gx', 'gy')
Inputs may be any that keep to these rules, and one draw needn't show every extreme that they name: `owners`: each request's positions form one run; every request owns at least one position and at most 16384, and some request owns exactly 16384. `expert_ids`: within each group of 64 requests no expert is named by more than 12 requests, a bound that some block reaches.
All inputs are finite; a program needn't handle non-finite values.
Results may differ from a plain program's by a relative error of at most 0.0075.
Values may be sent and summed in bfloat16 or wider, within the bound.
No kernel may reach another device: no remote copies, remote signals or barrier semaphores. Data moves between devices by JAX's collectives and lax.ppermute only.
A program may use at most 192 MiB of HBM per device.

v0:
```python
import jax
import jax.numpy as jnp
from jax import lax
from jax.sharding import PartitionSpec as P

D = 2560
QUERY_HEADS = 20
KEY_VALUE_HEADS = 4
HEAD_SIZE = 128
E = 64
TOPK = 6
CAPS = 12
minimal_score = -1e30
norm_epsilon = 1e-05


def merged(part, axis, combine):
    gathered = jax.tree.map(lambda a: lax.all_gather(a, axis), part)

    def take(source):
        return jax.tree.map(lambda a: lax.dynamic_index_in_dim(a, source, 0, False), gathered)

    return lax.fori_loop(
        1, lax.axis_size(axis), lambda source, state: combine(state, take(source)), take(0)
    )


def merge_partial(earlier_part, later_part):
    max_one, den_one, acc_one = earlier_part
    max_two, den_two, acc_two = later_part
    peak = jnp.maximum(max_one, max_two)
    scale_one = jnp.exp(max_one - peak)
    scale_two = jnp.exp(max_two - peak)
    return (
        peak,
        den_one * scale_one + den_two * scale_two,
        acc_one * scale_one[..., None] + acc_two * scale_two[..., None],
    )


def slot_ranks(flat_ids, num_experts):
    onehot = (flat_ids[..., None] == lax.iota(jnp.int32, num_experts)).astype(jnp.int32)
    earlier = jnp.cumsum(onehot, axis=-2) - onehot
    return jnp.sum(earlier * onehot, axis=-1)


def attend_local(queries, group_cached_keys, group_cached_values, owners):
    request_rows = queries.shape[0]
    query_heads_per_group = QUERY_HEADS // KEY_VALUE_HEADS
    positions = group_cached_keys.shape[0]
    block_length = min(positions, 512)
    block_count = positions // block_length
    key_block_list = group_cached_keys.reshape(
        block_count, block_length, KEY_VALUE_HEADS, HEAD_SIZE
    )
    value_block_list = group_cached_values.reshape(
        block_count, block_length, KEY_VALUE_HEADS, HEAD_SIZE
    )
    owner_blocks = owners.reshape(block_count, block_length)
    scaling = HEAD_SIZE ** (-0.5)
    request_ids = lax.iota(jnp.int32, request_rows)

    def visit_block(state_in, inputs):
        run_max, run_den, run_acc = state_in
        key_block, value_block, owning_block = inputs
        picked_experts = queries[owning_block].reshape(
            block_length, KEY_VALUE_HEADS, query_heads_per_group, HEAD_SIZE
        )
        scores = (
            jnp.einsum(
                "tkgd,tkd->tkg", picked_experts, key_block, preferred_element_type=jnp.float32
            )
            * scaling
        )
        member = owning_block[:, None] == request_ids[None, :]
        block_max = jnp.max(
            jnp.where(member[:, :, None, None], scores[:, None], minimal_score), axis=0
        )
        new_max = jnp.maximum(run_max, block_max)
        prob_block = jnp.exp(scores - new_max[owning_block]).astype(jnp.bfloat16)
        spread = jnp.where(
            member[:, :, None, None], prob_block[:, None], jnp.zeros((), jnp.bfloat16)
        )
        rescale = jnp.exp(run_max - new_max)
        run_den = run_den * rescale + jnp.sum(spread.astype(jnp.float32), axis=0)
        run_acc = run_acc * rescale[..., None] + jnp.einsum(
            "trkg,tkd->rkgd", spread, value_block, preferred_element_type=jnp.float32
        )
        return ((new_max, run_den, run_acc), None)

    initial = (
        jnp.full(
            (request_rows, KEY_VALUE_HEADS, query_heads_per_group), minimal_score, jnp.float32
        ),
        jnp.zeros((request_rows, KEY_VALUE_HEADS, query_heads_per_group), jnp.float32),
        jnp.zeros((request_rows, KEY_VALUE_HEADS, query_heads_per_group, HEAD_SIZE), jnp.float32),
    )
    return lax.scan(visit_block, initial, (key_block_list, value_block_list, owner_blocks))[0]


def expert_block(tokens, w_gate_up, w_down):
    hidden_units = w_down.shape[1]
    gate_up = jnp.einsum("sekd,edf->sekf", tokens, w_gate_up, preferred_element_type=jnp.float32)
    gate_up = lax.psum(gate_up, "gy")
    active = (jax.nn.silu(gate_up[..., :hidden_units]) * gate_up[..., hidden_units:]).astype(
        jnp.bfloat16
    )
    return jnp.einsum("sekf,efd->sekd", active, w_down, preferred_element_type=jnp.float32).astype(
        jnp.bfloat16
    )


def shards(
    queries,
    token_key_value,
    group_cached_keys,
    group_cached_values,
    owners,
    out_weight,
    residual,
    norm_gain,
    expert_ids,
    gate_logits,
    w_gate_up,
    w_down,
):
    request_rows = queries.shape[0]
    query_heads_per_group = QUERY_HEADS // KEY_VALUE_HEADS
    key_value_width = token_key_value.shape[1] // 2
    scaling = HEAD_SIZE ** (-0.5)
    run_max, run_den, run_acc = attend_local(
        queries, group_cached_keys[0], group_cached_values[0], owners[0]
    )
    query_head_rows = queries.reshape(
        request_rows, KEY_VALUE_HEADS, query_heads_per_group, HEAD_SIZE
    )
    appended_keys = token_key_value[:, :key_value_width].reshape(
        request_rows, KEY_VALUE_HEADS, HEAD_SIZE
    )
    appended_values = token_key_value[:, key_value_width:]
    own_score = (
        jnp.einsum(
            "rkgd,rkd->rkg", query_head_rows, appended_keys, preferred_element_type=jnp.float32
        )
        * scaling
    )
    run_max, run_den, run_acc = merged((run_max, run_den, run_acc), "gy", merge_partial)
    peak = jnp.maximum(run_max, own_score)
    rescale = jnp.exp(run_max - peak)
    own_prob = lax.optimization_barrier(jnp.exp(own_score - peak).astype(jnp.bfloat16)).astype(
        jnp.float32
    )
    denominator = run_den * rescale + own_prob
    incoming_values = appended_values.astype(jnp.float32).reshape(
        request_rows, KEY_VALUE_HEADS, 1, HEAD_SIZE
    )
    numerator = run_acc * rescale[..., None] + own_prob[..., None] * incoming_values
    attention = (
        (numerator / denominator[..., None])
        .astype(jnp.bfloat16)
        .reshape(request_rows, QUERY_HEADS * HEAD_SIZE)
    )
    projected = jnp.dot(attention, out_weight, preferred_element_type=jnp.float32)
    hidden = (residual.astype(jnp.float32) + projected).astype(jnp.bfloat16)
    hidden_f = hidden.astype(jnp.float32)
    squares = lax.psum(jnp.sum(hidden_f * hidden_f, axis=1), "gy")
    inv_rms = lax.rsqrt(squares / D + norm_epsilon)
    normed = (hidden_f * inv_rms[:, None] * norm_gain.astype(jnp.float32)[None, :]).astype(
        jnp.bfloat16
    )
    mixing = jax.nn.softmax(gate_logits, axis=-1)
    num_gx = lax.axis_size("gx")
    group_index = lax.axis_index("gx")
    per_row = w_gate_up.shape[0]
    columns_here = normed.shape[1]
    my_ids = lax.dynamic_slice_in_dim(
        expert_ids, group_index * request_rows, request_rows, 0
    ).reshape(-1)
    my_mix = lax.dynamic_slice_in_dim(mixing, group_index * request_rows, request_rows, 0)
    places = my_ids * CAPS + slot_ranks(my_ids, E)
    outgoing = (
        jnp.zeros((E * CAPS, columns_here), jnp.bfloat16)
        .at[places]
        .set(jnp.repeat(normed, TOPK, axis=0))
    )
    returned = lax.all_to_all(
        expert_block(
            lax.all_to_all(
                outgoing.reshape(num_gx, per_row, CAPS, columns_here),
                "gx",
                split_axis=0,
                concat_axis=0,
                tiled=True,
            ),
            w_gate_up,
            w_down,
        ),
        "gx",
        split_axis=0,
        concat_axis=0,
        tiled=True,
    )
    picked = (
        returned.reshape(E * CAPS, columns_here)[places]
        .astype(jnp.float32)
        .reshape(request_rows, TOPK, columns_here)
    )
    routed = jnp.sum(my_mix[..., None] * picked, axis=1)
    return hidden_f + routed


def solution(mesh):
    placed = (
        P("gx", None),
        P("gx", None),
        P("gx", "gy", None),
        P("gx", "gy", None),
        P("gx", "gy"),
        P(None, "gy"),
        P("gx", "gy"),
        P("gy"),
        P(),
        P(),
        P("gx", "gy", None),
        P("gx", None, "gy"),
    )
    return jax.shard_map(
        shards, mesh=mesh, in_specs=placed, out_specs=P("gx", "gy"), check_vma=False
    )
```

profile of v0, /device:TPU:0, one launch (start us, length us, event | category | flops | bytes accessed | tf_op | source)
XLA Modules:
  0.0 817.4 jit_solution(4890092526414652480)
XLA Ops:
  6.5 7.0 reshape.208
  13.6 7.0 reshape_squeeze.10
  22.4 178.0 %while.35 = (s32[]{:T(128)}, f32[64,4,5]{2,1,0:T(4,128)S(1)}, f32[64,4,5]{2,1,0:T(4,128)S(1)}, f32[64,4,5,128]{3,0,2,1:T(8,128)}, s32[8,512]{1,0:T(8,128)}, /*in...) while((s32[]{:T(128)}, f32[64,4,5]{2,1,0:T(4,128)S(1)}, ...), condition=%wide.region_3.4_spmd.clone, body=%wide.region_0.3_spmd.clone.sunk | while | flops 176462592 | bytes 21555320 | solution.py:98
  23.1 3.6 gather_fusion
  26.7 4.5 copy.169
  31.2 2.1 bitcast_convert_fusion.2
  34.9 2.3 multiply_reduce_fusion.4
  37.8 2.1 gather_fusion.1
  44.4 3.6 gather_fusion
  48.0 4.5 copy.169
  52.5 2.1 bitcast_convert_fusion.2
  56.2 2.3 multiply_reduce_fusion.4
  59.1 2.1 gather_fusion.1
  63.6 2.4 fusion.70
  66.8 3.6 gather_fusion
  70.4 4.5 copy.169
  74.9 2.1 bitcast_convert_fusion.2
  78.6 2.3 multiply_reduce_fusion.4
  81.5 2.1 gather_fusion.1
  86.0 2.4 fusion.70
  89.2 3.6 gather_fusion
  92.8 4.5 copy.169
  97.3 2.1 bitcast_convert_fusion.2
  101.0 2.3 multiply_reduce_fusion.4
  103.9 2.1 gather_fusion.1
  108.4 2.4 fusion.70
  111.6 3.6 gather_fusion
  115.2 4.5 copy.169
  119.7 2.1 bitcast_convert_fusion.2
  123.4 2.3 multiply_reduce_fusion.4
  126.3 2.1 gather_fusion.1
  130.8 2.4 fusion.70
  134.0 3.6 gather_fusion
  137.6 4.5 copy.169
  142.1 2.1 bitcast_convert_fusion.2
  145.8 2.3 multiply_reduce_fusion.4
  148.7 2.1 gather_fusion.1
  153.2 2.4 fusion.70
  156.4 3.6 gather_fusion
  160.0 4.5 copy.169
  164.5 2.1 bitcast_convert_fusion.2
  168.1 2.3 multiply_reduce_fusion.4
  171.1 2.1 gather_fusion.1
  175.6 2.4 fusion.70
  178.8 3.6 gather_fusion
  182.4 4.5 copy.169
  186.8 2.1 bitcast_convert_fusion.2
  190.5 2.3 multiply_reduce_fusion.4
  193.5 2.1 gather_fusion.1
  198.0 2.4 fusion.70
  202.2 38.6 %all-gather = f32[512,4,5]{2,1,0:T(4,128)S(1)} all-gather(f32[64,4,5]{2,1,0:T(4,128)S(1)} %get-tuple-element.232), channel_id=2, replica_groups=mesh['gx'=4,'gy'=8] {'gy'}, dimensions={0}, use_global_device_ids=true | all-gather | bytes 46080 | tf_op jit(solution)/shard_map/all_gather | solution.py:18
  240.9 35.2 %all-gather.1 = f32[512,4,5]{2,1,0:T(4,128)S(1)} all-gather(f32[64,4,5]{2,1,0:T(4,128)S(1)} %get-tuple-element.233), channel_id=3, replica_groups=mesh['gx'=4,'gy'=8] {'gy'}, dimensions={0}, use_global_device_ids=true | all-gather | bytes 46080 | tf_op jit(solution)/shard_map/all_gather | solution.py:18
  282.6 27.2 %all-gather.5.cloned.1.call-done = f32[512,4,5,128]{3,0,2,1:T(8,128)} async-done(((f32[64,4,5,128]{3,0,2,1:T(8,128)}), f32[512,4,5,128]{3,0,2,1:T(8,128)}) %all-gather.5.cloned.1.call-update) | async-done | bytes 5242896 | tf_op jit(solution)/shard_map/all_gather | solution.py:18
  311.4 20.6 %while.34 = (s32[]{:T(128)}, f32[64,4,5]{0,1,2:T(4,128)S(1)}, f32[64,4,5]{0,1,2:T(4,128)S(1)}, f32[64,4,5,128]{3,2,1,0:T(8,128)S(1)}, f32[8,64,4,5]{1,2,3,0:T(4,...) while((s32[]{:T(128)}, f32[64,4,5]{0,1,2:T(4,128)S(1)}, ...), condition=%wide.region_5.6_spmd, body=%wide.region_4.5_spmd.sunk | while | flops 499205 | bytes 3348631 | solution.py:23
  333.7 1.9 divide_convert_fusion
  336.7 19.3 %psum.14 = f32[64]{0:T(128)S(1)} all-reduce(f32[64]{0:T(128)S(1)} %get-tuple-element.365), channel_id=1, replica_groups=mesh['gx'=4,'gy'=8] {'gy'}, use_global_device_ids=true, to_apply=%region_12.13 | all-reduce | flops 64 | bytes 512 | tf_op jit(solution)/shard_map/psum | solution.py:166
  356.3 2.1 scatter_custom_fusion
  358.7 12.1 %all_to_all.10 = bf16[4,16,12,320]{3,1,2,0:T(8,128)(2,1)S(1)} all-to-all(bf16[4,16,12,320]{3,1,2,0:T(8,128)(2,1)S(1)} %copy.108), channel_id=1, replica_groups=mesh['gx'=4,'gy'=8] {'gx'}, dimensions={0} | all-to-all | bytes 983040 | tf_op jit(solution)/shard_map/all_to_all | solution.py:188
  370.8 16.6 %fusion.23 = f32[4,16,12,3072]{3,2,0,1:T(8,128)} fusion(bf16[16,320,3072]{2,1,0:T(8,128)(2,1)} %param.26, bf16[4,16,12,320]{3,1,2,0:T(8,128)(2,1)S(1)} %all_to_all.10), kind=kOutput, calls=%fused_computation.44 | convolution fusion | flops 1509949440 | bytes 41385984 | tf_op jit(solution)/shard_map/sekd,edf->sekf/dot_general | solution.py:103
  388.2 393.0 %all-reduce.2.cloned.1.call-done = f32[4,16,12,3072]{3,2,0,1:T(8,128)} async-done(((f32[4,16,12,3072]{3,2,0,1:T(8,128)}), f32[4,16,12,3072]{3,2,0,1:T(8,128)}) %all-reduce.2.cloned.1.call-update) | async-done | bytes 9437200 | tf_op jit(solution)/shard_map/psum | solution.py:104
  781.2 11.6 %fusion.34 = bf16[4,16,12,320]{3,2,0,1:T(8,128)(2,1)S(1)} fusion(bf16[16,1536,320]{1,2,0:T(8,128)(2,1)} %param.27, f32[4,16,12,3072]{3,2,0,1:T(8,128)} %all-reduce.2.cloned.1.call-done), kind=kOutput, calls=%fused_computation.49 | convolution fusion | flops 762298368 | bytes 25657344 | tf_op jit(solution)/shard_map/sekf,efd->sekd/dot_general | solution.py:108
  793.9 3.5 all-to-all-start.1
  797.7 9.2 %all-to-all-done.1 = bf16[4,16,12,320]{3,1,2,0:T(8,128)(2,1)S(1)} async-done(((bf16[4,16,12,320]{3,1,2,0:T(8,128)(2,1)}), bf16[4,16,12,320]{3,1,2,0:T(8,128)(2,1)S(1)}, u32[]{:S(2)}, u32[]{:S(2)}) %all-to-all-start.1) | async-done | bytes 491552 | tf_op jit(solution)/shard_map/all_to_all | solution.py:186
  807.4 2.1 gather_fusion.2
  (260 shorter events, 82.1 us)
Async XLA Ops:
  6.5 329.4 %copy-start = (bf16[2560,320]{0,1:T(8,128)(2,1)S(1)}, bf16[2560,320]{0,1:T(8,128)(2,1)}, u32[]{:S(2)}) copy-start(bf16[2560,320]{0,1:T(8,128)(2,1)} %param.21) | copy-start | bytes 4915204
  6.5 303.3 %all-gather.5.cloned.1.call-start = ((), (), s32[]{:S(2)}) async-start(), calls=%async_computation.3 | async-start | bytes 5898240 | tf_op jit(solution)/shard_map/all_gather | solution.py:18
  13.6 7.5 copy-start.6
  13.6 8.8 %copy-start.1 = (bf16[64,2560]{1,0:T(8,128)(2,1)S(1)}, bf16[64,2560]{1,0:T(8,128)(2,1)}, u32[]{:S(2)}) copy-start(bf16[64,2560]{1,0:T(8,128)(2,1)} %param.16) | copy-start | bytes 983044
  22.4 179.4 %copy-start.7 = (s32[256,6]{0,1:T(8,128)S(1)}, s32[256,6]{0,1:T(8,128)}, u32[]{:S(2)}) copy-start(s32[256,6]{0,1:T(8,128)} %param.24) | copy-start | bytes 18436
  200.4 78.9 %copy-start.3 = (bf16[64,1024]{1,0:T(8,128)(2,1)S(1)}, bf16[64,1024]{1,0:T(8,128)(2,1)}, u32[]{:S(2)}) copy-start(bf16[64,1024]{1,0:T(8,128)(2,1)} %param.17) | copy-start | bytes 393220
  200.5 80.5 %copy-start.8 = (bf16[320]{0:T(512)(128)(2,1)S(1)}, bf16[320]{0:T(512)(128)(2,1)}, u32[]{:S(2)}) copy-start(bf16[320]{0:T(512)(128)(2,1)} %param.23) | copy-start | bytes 1924
  200.5 580.7 %all-reduce.2.cloned.1.call-start = ((), (), s32[]{:S(2)}) async-start(), calls=%async_computation.2 | async-start | bytes 25165824 | tf_op jit(solution)/shard_map/psum | solution.py:104
  276.2 1.0 copy-start.2
  311.4 24.6 %copy-start.4 = (bf16[64,320]{1,0:T(8,128)(2,1)S(1)}, bf16[64,320]{1,0:T(8,128)(2,1)}, u32[]{:S(2)}) copy-start(bf16[64,320]{1,0:T(8,128)(2,1)} %param.22) | copy-start | bytes 122884
  387.4 0.7 copy-start.5
  793.9 13.0 %all-to-all-start.1 = ((bf16[4,16,12,320]{3,1,2,0:T(8,128)(2,1)}), bf16[4,16,12,320]{3,1,2,0:T(8,128)(2,1)S(1)}, u32[]{:S(2)}, u32[]{:S(2)}) async-start(bf16[4,16,12,320]{3,1,2,0:T(8,128)(2,1)} %copy.110), calls=%async_computation.1 | async-start | bytes 1179648 | tf_op jit(solution)/shard_map/all_to_all | solution.py:186
Sparse Core Ops, SparseCore 0:
  200.6 109.1 all-gather.4
  387.6 393.5 all-reduce.1
where the time goes:
time: 821 us; the launch traced here: 817 us
  waiting for transfers between devices  429 us (52%)
  local copies, waits for them, and re-layouts  151 us (18%)
  blocking collectives  105 us (13%)
  other arithmetic  64.6 us (8%)
  matrix products  48.9 us (6%)
  between operations  13.7 us (2%)
    psum x1, waiting for transfers between devices, expert_block(): gate_up = lax.psum(gate_up, 'gy')  393 us
    all_gather x2, blocking collectives, merged(): gathered = jax.tree.map(lambda a: lax.all_gather(a, axis), part)  73.9 us
    while x24, local copies, waits for them, and re-layouts  48.4 us
    while x16, other arithmetic  35.7 us
    gather x8, local copies, waits for them, and re-layouts, visit_block(): queries[owning_block]  28.5 us
    all_gather x1, waiting for transfers between devices, merged(): gathered = jax.tree.map(lambda a: lax.all_gather(a, axis), part)  27.2 us
    gather x16, local copies, waits for them, and re-layouts, visit_block(): prob_block = jnp.exp(scores - new_max[owning_block]).astype(jnp.bfloat16)  19.4 us
    psum x1, blocking collectives, shards(): squares = lax.psum(jnp.sum(hidden_f * hidden_f, axis=1), 'gy')  19.3 us
  transfers between devices with their start and end apart: 3, of which 3 were waited for; matrix products, arithmetic and copies ran while one was open for 1% of the time, Pallas kernels for 0%

commit v1 on v0

--- a/solution.py
+++ b/solution.py
@@ -101,7 +101,9 @@
 def expert_block(tokens, w_gate_up, w_down):
     hidden_units = w_down.shape[1]
     gate_up = jnp.einsum("sekd,edf->sekf", tokens, w_gate_up, preferred_element_type=jnp.float32)
-    gate_up = lax.psum(gate_up, "gy")
+    gate_up = gate_up
+    for hop in (1, 2, 4):
+        gate_up = gate_up + lax.ppermute(gate_up, "gy", [(dev, dev ^ hop) for dev in range(8)])
     active = (jax.nn.silu(gate_up[..., :hidden_units]) * gate_up[..., hidden_units:]).astype(
         jnp.bfloat16
     )

time: 821 us -> 1320 us (1.61)
  waiting for transfers between devices: 429 us -> 851 us
  other arithmetic: 64.6 us -> 113 us
    ppermute x0 -> x3, waiting for transfers between devices: none -> 815 us  [expert_block(): lax.ppermute(gate_up, 'gy', [(dev, dev ^ hop) for dev in range(8)])]
    psum x1 -> x0, waiting for transfers between devices: 393 us -> none  [expert_block(): gate_up = lax.psum(gate_up, 'gy')]
    add x0 -> x3, other arithmetic: none -> 43 us  [expert_block(): gate_up + lax.ppermute(gate_up, 'gy', [(dev, dev ^ hop) for dev in range(...]
  transfers between devices with their start and end apart: 3 -> 5, of which waited for: 3 -> 5; matrix products, arithmetic and copies ran while one was open for 1% -> 1% of each run, Pallas kernels for 0% -> 0%
where the time goes in v1:
time: 1320 us; the launch traced here: 1310 us
  waiting for transfers between devices  851 us (64%)
  local copies, waits for them, and re-layouts  160 us (12%)
  blocking collectives  117 us (9%)
  other arithmetic  113 us (9%)
  matrix products  48.3 us (4%)
  between operations  14.1 us (1%)
    ppermute x3, waiting for transfers between devices, expert_block(): lax.ppermute(gate_up, 'gy', [(dev, dev ^ hop) for dev in range(8)])  815 us
    all_gather x2, blocking collectives, merged(): gathered = jax.tree.map(lambda a: lax.all_gather(a, axis), part)  74 us
    while x24, local copies, waits for them, and re-layouts  48.4 us
    add x3, other arithmetic, expert_block(): gate_up + lax.ppermute(gate_up, 'gy', [(dev, dev ^ hop) for dev in range(...  43 us
    while x16, other arithmetic  35.7 us
    psum x1, blocking collectives, shards(): squares = lax.psum(jnp.sum(hidden_f * hidden_f, axis=1), 'gy')  30.7 us
    gather x8, local copies, waits for them, and re-layouts, visit_block(): queries[owning_block]  28.5 us
    all_gather x1, waiting for transfers between devices, merged(): gathered = jax.tree.map(lambda a: lax.all_gather(a, axis), part)  27.1 us
  transfers between devices with their start and end apart: 5, of which 5 were waited for; matrix products, arithmetic and copies ran while one was open for 1% of the time, Pallas kernels for 0%

profile of v1, /device:TPU:0, one launch (start us, length us, event | category | flops | bytes accessed | tf_op | source)
XLA Modules:
  0.0 1308.7 jit_solution(2745890074976167250)
XLA Ops:
  6.5 7.0 reshape.208
  13.6 7.0 reshape_squeeze.10
  22.4 178.1 %while.35 = (s32[]{:T(128)}, f32[64,4,5]{2,1,0:T(4,128)S(1)}, f32[64,4,5]{2,1,0:T(4,128)S(1)}, f32[64,4,5,128]{3,0,2,1:T(8,128)}, s32[8,512]{1,0:T(8,128)}, /*in...) while((s32[]{:T(128)}, f32[64,4,5]{2,1,0:T(4,128)S(1)}, ...), condition=%wide.region_3.4_spmd.clone, body=%wide.region_0.3_spmd.clone.sunk | while | flops 176462592 | bytes 21555320 | solution.py:98
  23.1 3.6 gather_fusion
  26.7 4.5 copy.187
  31.2 2.1 bitcast_convert_fusion.2
  34.9 2.3 multiply_reduce_fusion.4
  37.8 2.1 gather_fusion.1
  44.4 3.6 gather_fusion
  48.0 4.5 copy.187
  52.5 2.1 bitcast_convert_fusion.2
  56.2 2.3 multiply_reduce_fusion.4
  59.1 2.1 gather_fusion.1
  63.6 2.4 fusion.66
  66.8 3.6 gather_fusion
  70.4 4.5 copy.187
  74.9 2.1 bitcast_convert_fusion.2
  78.6 2.3 multiply_reduce_fusion.4
  86.0 2.4 fusion.66
  89.2 3.6 gather_fusion
  92.8 4.5 copy.187
  97.3 2.1 bitcast_convert_fusion.2
  101.0 2.3 multiply_reduce_fusion.4
  108.4 2.4 fusion.66
  111.6 3.6 gather_fusion
  115.2 4.5 copy.187
  119.7 2.1 bitcast_convert_fusion.2
  123.4 2.3 multiply_reduce_fusion.4
  130.8 2.4 fusion.66
  134.0 3.6 gather_fusion
  137.6 4.5 copy.187
  142.1 2.1 bitcast_convert_fusion.2
  145.8 2.3 multiply_reduce_fusion.4
  153.2 2.4 fusion.66
  156.4 3.6 gather_fusion
  160.0 4.5 copy.187
  164.5 2.1 bitcast_convert_fusion.2
  168.1 2.3 multiply_reduce_fusion.4
  175.6 2.4 fusion.66
  178.8 3.6 gather_fusion
  182.4 4.5 copy.187
  186.8 2.1 bitcast_convert_fusion.2
  190.5 2.3 multiply_reduce_fusion.4
  198.0 2.4 fusion.66
  202.1 38.6 %all-gather = f32[512,4,5]{2,1,0:T(4,128)S(1)} all-gather(f32[64,4,5]{2,1,0:T(4,128)S(1)} %get-tuple-element.232), channel_id=2, replica_groups=mesh['gx'=4,'gy'=8] {'gy'}, dimensions={0}, use_global_device_ids=true | all-gather | bytes 46080 | tf_op jit(solution)/shard_map/all_gather | solution.py:18
  240.9 35.4 %all-gather.1 = f32[512,4,5]{2,1,0:T(4,128)S(1)} all-gather(f32[64,4,5]{2,1,0:T(4,128)S(1)} %get-tuple-element.233), channel_id=3, replica_groups=mesh['gx'=4,'gy'=8] {'gy'}, dimensions={0}, use_global_device_ids=true | all-gather | bytes 46080 | tf_op jit(solution)/shard_map/all_gather | solution.py:18
  282.7 27.1 %all-gather.5.cloned.1.call-done = f32[512,4,5,128]{3,0,2,1:T(8,128)} async-done(((f32[64,4,5,128]{3,0,2,1:T(8,128)}), f32[512,4,5,128]{3,0,2,1:T(8,128)}) %all-gather.5.cloned.1.call-update) | async-done | bytes 5242896 | tf_op jit(solution)/shard_map/all_gather | solution.py:18
  311.3 20.6 %while.34 = (s32[]{:T(128)}, f32[64,4,5]{0,1,2:T(4,128)S(1)}, f32[64,4,5]{0,1,2:T(4,128)S(1)}, f32[64,4,5,128]{3,2,1,0:T(8,128)S(1)}, f32[8,64,4,5]{1,2,3,0:T(4,...) while((s32[]{:T(128)}, f32[64,4,5]{0,1,2:T(4,128)S(1)}, ...), condition=%wide.region_5.6_spmd, body=%wide.region_4.5_spmd.sunk | while | flops 499205 | bytes 3348631 | solution.py:23
  336.6 30.7 %psum.7 = f32[64]{0:T(128)S(1)} all-reduce(f32[64]{0:T(128)S(1)} %get-tuple-element.365), channel_id=1, replica_groups=mesh['gx'=4,'gy'=8] {'gy'}, use_global_device_ids=true, to_apply=%region_12.13 | all-reduce | flops 64 | bytes 512 | tf_op jit(solution)/shard_map/psum | solution.py:168
  367.7 2.1 scatter_custom_fusion
  370.1 12.3 all_to_all.10
  382.4 16.7 %fusion.19 = f32[16,4,12,3072]{3,2,1,0:T(8,128)} fusion(bf16[16,320,3072]{2,1,0:T(8,128)(2,1)} %param.26, bf16[4,16,12,320]{3,1,2,0:T(8,128)(2,1)S(1)} %all_to_all.10), kind=kOutput, calls=%fused_computation.40 | convolution fusion | flops 1509949440 | bytes 41385984 | tf_op jit(solution)/shard_map/sekd,edf->sekf/dot_general | solution.py:103
  399.1 10.0 copy.166
  409.2 204.7 %collective-permute-done = f32[4,16,12,3072]{3,1,2,0:T(8,128)} collective-permute-done((f32[4,16,12,3072]{3,1,2,0:T(8,128)S(1)}, f32[4,16,12,3072]{3,1,2,0:T(8,128)}, u32[]{:S(2)}, u32[]{:S(2)}) %collective-permute-start) | collective-permute-done | bytes 9437216 | tf_op jit(solution)/shard_map/ppermute | solution.py:106
  613.9 17.4 %fusion.56 = f32[4,16,12,3072]{3,1,2,0:T(8,128)} fusion(f32[4,16,12,3072]{3,1,2,0:T(8,128)} %collective-permute-done, f32[16,4,12,3072]{3,2,1,0:T(8,128)} %fusion.19), kind=kLoop, calls=%fused_computation.87 | loop fusion | flops 2359296 | bytes 28311552 | tf_op jit(solution)/shard_map/add | solution.py:106
  631.4 204.0 %collective-permute-done.1 = f32[4,16,12,3072]{3,1,2,0:T(8,128)} collective-permute-done((f32[4,16,12,3072]{3,1,2,0:T(8,128)}, f32[4,16,12,3072]{3,1,2,0:T(8,128)}, u32[]{:S(2)}, u32[]{:S(2)}) %collective-permute-start.1) | collective-permute-done | bytes 9437216 | tf_op jit(solution)/shard_map/ppermute | solution.py:106
  835.4 12.8 add.147
  848.2 406.2 %collective-permute-done.2 = f32[4,16,12,3072]{3,1,2,0:T(8,128)} collective-permute-done((f32[4,16,12,3072]{3,1,2,0:T(8,128)}, f32[4,16,12,3072]{3,1,2,0:T(8,128)}, u32[]{:S(2)}, u32[]{:S(2)}) %collective-permute-start.2) | collective-permute-done | bytes 9437216 | tf_op jit(solution)/shard_map/ppermute | solution.py:106
  1254.4 12.8 add.148
  1267.1 5.5 fusion.23
  1272.7 11.0 fusion.30
  1284.9 3.5 all-to-all-start.1
  1288.6 9.2 all-to-all-done.1
  1298.3 2.1 gather_fusion.2
  (270 shorter events, 95.8 us)
Async XLA Ops:
  6.5 329.4 %copy-start = (bf16[2560,320]{0,1:T(8,128)(2,1)S(1)}, bf16[2560,320]{0,1:T(8,128)(2,1)}, u32[]{:S(2)}) copy-start(bf16[2560,320]{0,1:T(8,128)(2,1)} %param.21) | copy-start | bytes 4915204
  6.5 303.2 %all-gather.5.cloned.1.call-start = ((), (), s32[]{:S(2)}) async-start(), calls=%async_computation.2 | async-start | bytes 5898240 | tf_op jit(solution)/shard_map/all_gather | solution.py:18
  13.6 7.5 copy-start.7
  13.6 8.8 copy-start.2
  22.4 179.3 %copy-start.8 = (s32[256,6]{0,1:T(8,128)S(1)}, s32[256,6]{0,1:T(8,128)}, u32[]{:S(2)}) copy-start(s32[256,6]{0,1:T(8,128)} %param.24) | copy-start | bytes 18436
  200.4 78.9 %copy-start.4 = (bf16[64,1024]{1,0:T(8,128)(2,1)S(1)}, bf16[64,1024]{1,0:T(8,128)(2,1)}, u32[]{:S(2)}) copy-start(bf16[64,1024]{1,0:T(8,128)(2,1)} %param.17) | copy-start | bytes 393220
  200.5 80.6 %copy-start.9 = (bf16[320]{0:T(512)(128)(2,1)S(1)}, bf16[320]{0:T(512)(128)(2,1)}, u32[]{:S(2)}) copy-start(bf16[320]{0:T(512)(128)(2,1)} %param.23) | copy-start | bytes 1924
  276.2 1.0 copy-start.3
  311.3 24.6 %copy-start.5 = (bf16[64,320]{1,0:T(8,128)(2,1)S(1)}, bf16[64,320]{1,0:T(8,128)(2,1)}, u32[]{:S(2)}) copy-start(bf16[64,320]{1,0:T(8,128)(2,1)} %param.22) | copy-start | bytes 122884
  409.2 204.8 %collective-permute-start = (f32[4,16,12,3072]{3,1,2,0:T(8,128)S(1)}, f32[4,16,12,3072]{3,1,2,0:T(8,128)}, u32[]{:S(2)}, u32[]{:S(2)}) collective-permute-start(f32[4,16,12,3072]{3,1,2,0:T(8,128)S(1)} %bitcast.111), channel_id=1, source_target_pairs={{0,1},{1,0},{2,3},{3,2},{4,5},{5,4},{6,7},{7,6},{8,9},{9,8},{10,11... | collective-permute-start | bytes 28311560 | tf_op jit(solution)/shard_map/ppermute | solution.py:106
  631.4 216.8 %copy-start.6 = (f32[256,6]{0,1:T(8,128)S(1)}, f32[256,6]{0,1:T(8,128)}, u32[]{:S(2)}) copy-start(f32[256,6]{0,1:T(8,128)} %param.25) | copy-start | bytes 18436
  631.4 204.0 %collective-permute-start.1 = (f32[4,16,12,3072]{3,1,2,0:T(8,128)}, f32[4,16,12,3072]{3,1,2,0:T(8,128)}, u32[]{:S(2)}, u32[]{:S(2)}) collective-permute-start(f32[4,16,12,3072]{3,1,2,0:T(8,128)} %fusion.56), channel_id=1, source_target_pairs={{0,2},{1,3},{2,0},{3,1},{4,6},{5,7},{6,4},{7,5},{8,10},{9,11},{10,... | collective-permute-start | bytes 28311560 | tf_op jit(solution)/shard_map/ppermute | solution.py:106
  848.1 406.2 %collective-permute-start.2 = (f32[4,16,12,3072]{3,1,2,0:T(8,128)}, f32[4,16,12,3072]{3,1,2,0:T(8,128)}, u32[]{:S(2)}, u32[]{:S(2)}) collective-permute-start(f32[4,16,12,3072]{3,1,2,0:T(8,128)} %add.147), channel_id=1, source_target_pairs={{0,4},{1,5},{2,6},{3,7},{4,0},{5,1},{6,2},{7,3},{8,12},{9,13},{10,... | collective-permute-start | bytes 28311560 | tf_op jit(solution)/shard_map/ppermute | solution.py:106
  1283.7 17.8 %copy-start.1 = (bf16[2560,320]{0,1:T(8,128)(2,1)S(1)}, bf16[2560,320]{0,1:T(8,128)(2,1)}, u32[]{:S(2)}) copy-start(bf16[2560,320]{0,1:T(8,128)(2,1)} %param.21) | copy-start | bytes 4915204
  1284.9 13.0 all-to-all-start.1
Sparse Core Ops, SparseCore 0:
  200.6 109.1 all-gather.4
